TPU v7x, 512 devices: a whole 4x4x16 slice. The times are simulated.
512 devices in a mesh: row: 16 (over y, x), col: 16 (over z), depth: 2 (over core).
Axes of the slice: x: 4, y: 4, z: 16, core: 2. Of those that a mesh axis runs over, the one named last changes fastest.
Arguments:
- left_store: float32 [16, 2, 16, 2, 64, 1024], P('row', 'depth', 'col'), may hold values from -6 to 6
- left_home: int32 [16, 2, 16], P('row', 'depth'), may hold values from 0 to 15, each once within a row
- up_store: float32 [16, 2, 16, 2, 64, 1024], P('col', 'depth', 'row'), may hold values from -0.3125 to 0.3125
- up_home: int32 [16, 2, 16], P('col', 'depth'), may hold values from 0 to 15, each once within a row
- targets: int32 [16, 16, 2], P('row', 'col'), may hold values from 0 to 63, as said below
- sketch: float32 [16, 16, 2, 64, 1024], P('row', 'col'), may hold values from -0.1875 to 0.1875
Outputs:
- basis: float32 [16, 16, 2, 64, 1024], P('row', 'col', 'depth')
- weights: float32 [16, 16, 2, 64, 1024], P('row', 'col', 'depth')
Inputs may be any that keep to these rules, and one draw needn't show every extreme that they name: `left_home`: for each row and depth index the entries are the store positions 0 to 15, each once. `up_home`: for each col and depth index the entries are the store positions 0 to 15, each once. `targets`: the 2 entries of one row and col index are distinct.
All inputs are finite; a program needn't handle non-finite values.
Results may differ from a plain program's by a relative error of at most 0.0003.
Values sent between devices are 32-bit elements; how exact they have to be, the bound alone decides.
No kernel may reach another device: no remote copies, remote signals or barrier semaphores. Data moves between devices by JAX's collectives and lax.ppermute only.
A program may use at most 128 MiB of HBM per device.

v0:
```python
import math
import jax
import jax.numpy as jnp
from jax import lax
from jax.sharding import PartitionSpec as P

KD = 2
RB = 8
CB = 8


def split_up(shard, dim, devices):
    before, after = (shard.shape[:dim], shard.shape[dim + 1 :])
    return jnp.moveaxis(shard.reshape(*before, devices, -1, *after), dim, 0)


def sent_and_summed(shard, axis, dim):
    devices = lax.axis_size(axis)
    pieces = lax.all_to_all(split_up(shard, dim, devices), axis, 0, 0, tiled=True)
    return jnp.sum(pieces, axis=0)


def laid_out(pieces, dim):
    pieces = jnp.moveaxis(pieces, 0, dim)
    shape = pieces.shape
    return pieces.reshape(*shape[:dim], shape[dim] * shape[dim + 1], *shape[dim + 2 :])


def copy_for_each(shard, axis):
    devices = lax.axis_size(axis)
    return lax.all_to_all(
        jnp.broadcast_to(shard[None], (devices, *shard.shape)), axis, 0, 0, tiled=True
    )


def gathered_copies(shard, axis, dim):
    return laid_out(copy_for_each(shard, axis), dim)


def orthonormal(sample):
    gram_mat = jnp.einsum("pat,pbt->pab", sample, sample, precision=lax.Precision.HIGHEST)
    factor_low = jnp.linalg.cholesky(gram_mat)
    return lax.linalg.triangular_solve(factor_low, sample, left_side=True, lower=True)


def shards(left_store, left_home, up_store, up_home, targets, sketch):
    high = lax.Precision.HIGHEST
    left_local = left_store[0, 0]
    up_local = up_store[0, 0]
    left_table = left_home[0, 0]
    up_table = up_home[0, 0]
    left_all = lax.all_gather(left_local, "col", axis=0, tiled=True)
    up_all = lax.all_gather(up_local, "row", axis=0, tiled=True)
    left_pairs = jnp.take(left_all, left_table, axis=0)
    up_pairs = jnp.take(up_all, up_table, axis=0)
    chosen = targets[0, 0]
    block_row = chosen // CB
    block_col = chosen % CB
    row_pairs = jnp.take(left_pairs.reshape((RB, KD) + left_local.shape[1:]), block_row, axis=0)
    col_pairs = jnp.take(up_pairs.reshape((CB, KD) + up_local.shape[1:]), block_col, axis=0)
    row_basis = row_pairs[:, :, 0]
    row_coef = row_pairs[:, :, 1]
    col_coef = col_pairs[:, :, 0]
    col_basis = col_pairs[:, :, 1]
    test_rows = sketch[0, 0]
    middle = jnp.einsum("pkat,pkbt->pkab", row_coef, col_coef, precision=high)
    test_side = jnp.einsum("pat,pkbt->pkab", test_rows, col_basis, precision=high)
    folded = jnp.einsum("pkab,pkcb->pkac", test_side, middle, precision=high)
    sample_part = jnp.einsum("pkac,pkct->pat", folded, row_basis, precision=high)
    own_sketch = sent_and_summed(sample_part, "depth", 0)
    own_basis = orthonormal(own_sketch)
    bases = gathered_copies(own_basis, "depth", 0)
    inner_prod = jnp.einsum("pat,pkct->pkac", bases, row_basis, precision=high)
    turned = jnp.einsum("pkac,pkcb->pkab", inner_prod, middle, precision=high)
    project_part = jnp.einsum("pkab,pkbt->pat", turned, col_basis, precision=high)
    projected = sent_and_summed(project_part, "depth", 0)
    root_tile = math.sqrt(test_rows.shape[-1])
    return ((own_basis * root_tile)[None, None], (projected / root_tile)[None, None])


def solution(mesh):
    return jax.shard_map(
        shards,
        mesh=mesh,
        in_specs=(
            P("row", "depth", "col", None, None, None),
            P("row", "depth", None),
            P("col", "depth", "row", None, None, None),
            P("col", "depth", None),
            P("row", "col", None),
            P("row", "col", None, None, None),
        ),
        out_specs=(P("row", "col", "depth", None, None), P("row", "col", "depth", None, None)),
        check_vma=False,
    )
```

profile of v0, /device:TPU:1, one launch (start us, length us, event | category | flops | bytes accessed | tf_op | source)
XLA Modules:
  0.0 273.3 jit_solution(12288357249461976770)
XLA Ops:
  7.2 0.0 copy-start
  7.2 0.0 all-gather.7.cloned.1.call-start
  7.2 0.7 all-gather.7.cloned.1.call-update
  7.9 0.0 all-gather.5.cloned.1.call-start
  8.0 0.7 all-gather.5.cloned.1.call-update
  8.7 0.7 compare_select_fusion.1
  9.3 0.7 compare_and_fusion
  10.0 0.7 compare_select_fusion.3
  10.7 0.7 compare_and_fusion.1
  11.4 0.7 compare_and_fusion.3
  12.0 109.1 %all-gather.7.cloned.1.call-done = f32[16,1,1,2,64,1024]{5,4,3,2,1,0:T(8,128)} async-done(((f32[1,1,1,2,64,1024]{5,4,3,2,1,0:T(8,128)}), f32[16,1,1,2,64,1024]{5,4,3,2,1,0:T(8,128)}) %all-gather.7.cloned.1.call-update) | async-done | bytes 8388624 | tf_op jit(solution)/shard_map/all_gather | solution.py:52
  121.1 7.7 %gather_fusion.2 = f32[16,2,64,1024]{3,2,1,0:T(8,128)} fusion(f32[16,2,64,1024]{3,2,1,0:T(8,128)} %bitcast.97, s32[1024]{0:T(1024)S(1)} %pad_clamp_fusion.1), kind=kCustom, calls=%fused_computation.2.clone | custom fusion | bytes 16777280 | tf_op jit(solution)/shard_map/jit(_take)/gather | solution.py:54
  128.8 8.6 %broadcast_select_fusion = f32[16,2,64,1024]{3,2,1,0:T(8,128)} fusion(f32[16,2,64,1024]{3,2,1,0:T(8,128)} %gather_fusion.2, pred[16]{0:T(512)(128)(4,1)S(1)} %compare_and_fusion.1), kind=kLoop, calls=%fused_computation.4 | loop fusion | flops 2097152 | bytes 16777232 | tf_op jit(solution)/shard_map/jit(_take)/select_n | solution.py:54
  137.4 5.8 %gather_fusion.3 = f32[2,2,2,64,1024]{4,3,2,1,0:T(8,128)} fusion(f32[8,2,2,64,1024]{4,3,2,1,0:T(8,128)} %bitcast.94, s32[1024]{0:T(1024)S(1)} %pad_clamp_fusion), kind=kCustom, calls=%fused_computation.3.clone | custom fusion | bytes 4194312 | tf_op jit(solution)/shard_map/jit(_take)/gather | solution.py:59
  143.2 65.0 %all-gather.5.cloned.1.call-done = f32[16,1,1,2,64,1024]{5,4,3,2,1,0:T(8,128)} async-done(((f32[1,1,1,2,64,1024]{5,4,3,2,1,0:T(8,128)}), f32[16,1,1,2,64,1024]{5,4,3,2,1,0:T(8,128)}) %all-gather.5.cloned.1.call-update) | async-done | bytes 8388624 | tf_op jit(solution)/shard_map/all_gather | solution.py:53
  208.2 7.7 %gather_fusion = f32[16,2,64,1024]{3,2,1,0:T(8,128)} fusion(f32[16,2,64,1024]{3,2,1,0:T(8,128)} %bitcast.96, s32[1024]{0:T(1024)S(1)} %pad_clamp_fusion.3), kind=kCustom, calls=%fused_computation.clone | custom fusion | bytes 16777280 | tf_op jit(solution)/shard_map/jit(_take)/gather | solution.py:55
  215.8 8.6 %broadcast_select_fusion.1 = f32[16,2,64,1024]{3,2,1,0:T(8,128)} fusion(f32[16,2,64,1024]{3,2,1,0:T(8,128)} %gather_fusion, pred[16]{0:T(512)(128)(4,1)S(1)} %compare_and_fusion.3), kind=kLoop, calls=%fused_computation.5 | loop fusion | flops 2097152 | bytes 16777232 | tf_op jit(solution)/shard_map/jit(_take)/select_n | solution.py:55
  224.4 5.4 %gather_fusion.1 = f32[2,2,2,64,1024]{4,3,2,1,0:T(8,128)} fusion(f32[8,2,2,64,1024]{4,3,2,1,0:T(8,128)} %bitcast.95, s32[1024]{0:T(1024)S(1)} %pad_clamp_fusion.2), kind=kCustom, calls=%fused_computation.1.clone | custom fusion | bytes 4194312 | tf_op jit(solution)/shard_map/jit(_take)/gather | solution.py:60
  229.9 2.8 %copy_select_fusion = (f32[2,2,2,64,1024]{4,3,1,0,2:T(8,128)S(1)}, f32[2,2,2,64,1024]{4,3,1,0,2:T(8,128)S(1)}) fusion(f32[2,2,2,64,1024]{4,3,2,1,0:T(8,128)} %gather_fusion.3, pred[2]{0:T(512)(128)(4,1)S(1)} %get-tuple-element.4, f32[2,2,2,64,1024]{4,3,2,1,0:T(8,128)} %gather_fusion.1, pred[2]{0:T(512)(128)(4,1)S(1)} %get-tuple-element.8), kind=kLoop, calls=%fused_computation.6 | loop fusion | flops 1048576 | bytes 8388612 | tf_op jit(solution)/shard_map/jit(_take)/select_n | solution.py:59
  232.6 0.0 copy-start.1
  232.6 0.0 copy-done
  232.7 1.6 fusion.1
  234.3 1.1 fusion
  235.4 0.3 fusion.9
  235.7 0.0 copy-done.1
  235.7 0.7 convolution_bitcast_fusion.1
  236.4 4.6 %all_to_all.15 = f32[2,1,64,1024]{3,2,1,0:T(8,128)S(1)} all-to-all(f32[2,1,64,1024]{3,2,1,0:T(8,128)S(1)} %convolution_bitcast_fusion.1), channel_id=1, replica_groups=mesh['row'=16,'col'=16,'depth'=2] {'depth'}, dimensions={0} | all-to-all | bytes 1048576 | tf_op jit(solution)/shard_map/all_to_all | solution.py:19
  241.1 0.4 fusion.10
  241.4 0.1 copy.27
  241.5 5.8 %custom-call.7 = f32[1,64,64]{2,1,0:T(8,128)S(1)} custom-call(f32[1,64,64]{2,1,0:T(8,128)S(1)} %fusion.6), custom_call_target="Cholesky" | custom-call | tf_op jit(solution)/shard_map/jit(cholesky)/cholesky | solution.py:42
  247.4 0.6 compare_reduce_fusion
  248.1 0.7 fusion.5
  248.7 4.9 %custom-call.8 = f32[1,1,64,64]{2,3,1,0:T(8,128)S(1)} custom-call(f32[1,1,64,64]{3,2,1,0:T(8,128)S(1)} %fusion.5), custom_call_target="InvertDiagBlocksLowerTriangular" | custom-call | tf_op jit(solution)/shard_map/triangular_solve | solution.py:43
  253.6 0.0 copy-start.2
  253.6 0.4 fusion.7
  254.1 0.7 multiply_bitcast_fusion.1
  254.8 4.2 %all_to_all.16 = f32[2,1,64,1024]{3,2,1,0:T(8,128)S(1)} all-to-all(f32[2,1,64,1024]{3,2,1,0:T(8,128)S(1)} %broadcast_in_dim.33), channel_id=1, replica_groups=mesh['row'=16,'col'=16,'depth'=2] {'depth'}, dimensions={0} | all-to-all | bytes 1048576 | tf_op jit(solution)/shard_map/all_to_all | solution.py:31
  259.0 0.0 copy-done.2
  259.0 1.6 fusion.2
  260.6 0.3 fusion.11
  260.9 0.7 convolution_bitcast_fusion
  261.6 4.2 %all_to_all.17 = f32[2,1,64,1024]{3,2,1,0:T(8,128)S(1)} all-to-all(f32[2,1,64,1024]{3,2,1,0:T(8,128)S(1)} %convolution_bitcast_fusion), channel_id=1, replica_groups=mesh['row'=16,'col'=16,'depth'=2] {'depth'}, dimensions={0} | all-to-all | bytes 1048576 | tf_op jit(solution)/shard_map/all_to_all | solution.py:19
  265.8 0.7 multiply_bitcast_fusion
  (9 shorter events, 0.2 us)
Async XLA Ops:
  7.2 225.5 %copy-start = (f32[1,1,2,64,1024]{4,3,2,1,0:T(8,128)S(1)}, f32[1,1,2,64,1024]{4,3,2,1,0:T(8,128)}, u32[]{:S(2)}) copy-start(f32[1,1,2,64,1024]{4,3,2,1,0:T(8,128)} %param.15) | copy-start | bytes 1572868
  7.2 113.9 %all-gather.7.cloned.1.call-start = ((), (), s32[]{:S(2)}) async-start(), calls=%async_computation.4 | async-start | bytes 8912896 | tf_op jit(solution)/shard_map/all_gather | solution.py:52
  7.9 200.3 %all-gather.5.cloned.1.call-start = ((), (), s32[]{:S(2)}) async-start(), calls=%async_computation.3 | async-start | bytes 8912896 | tf_op jit(solution)/shard_map/all_gather | solution.py:53
  232.6 3.1 %copy-start.1 = (f32[2,2,2,64,1024]{4,3,1,0,2:T(8,128)}, f32[2,2,2,64,1024]{4,3,1,0,2:T(8,128)S(1)}, u32[]{:S(2)}) copy-start(f32[2,2,2,64,1024]{4,3,1,0,2:T(8,128)S(1)} %get-tuple-element.10) | copy-start | bytes 6291460
  253.6 5.4 %copy-start.2 = (f32[2,2,2,64,1024]{4,3,1,0,2:T(8,128)S(1)}, f32[2,2,2,64,1024]{4,3,1,0,2:T(8,128)}, u32[]{:S(2)}) copy-start(f32[2,2,2,64,1024]{4,3,1,0,2:T(8,128)} %copy-done.1) | copy-start | bytes 6291460
Sparse Core Ops, SparseCore 0:
  10.1 110.9 all-gather.6
  124.1 84.0 all-gather.4
where the time goes:
time: 274 us; the launch traced here: 273 us
  waiting for transfers between devices  175 us (64%)
  other arithmetic  36.9 us (13%)
  local copies, waits for them, and re-layouts  26.7 us (10%)
  between operations  14.2 us (5%)
  blocking collectives  12.9 us (5%)
  matrix products  7.07 us (3%)
    all_gather x1, waiting for transfers between devices, shards(): left_all = lax.all_gather(left_local, 'col', axis=0, tiled=True)  109 us
    all_gather x1, waiting for transfers between devices, shards(): up_all = lax.all_gather(up_local, 'row', axis=0, tiled=True)  65 us
    select_n x2, other arithmetic, shards(): left_pairs = jnp.take(left_all, left_table, axis=0)  9.27 us
    select_n x2, other arithmetic, shards(): up_pairs = jnp.take(up_all, up_table, axis=0)  9.26 us
    all_to_all x2, blocking collectives, sent_and_summed(): lax.all_to_all(split_up(shard, dim, devices), axis, 0, 0, tiled=True)  8.78 us
    gather x1, local copies, waits for them, and re-layouts, shards(): left_pairs = jnp.take(left_all, left_table, axis=0)  7.68 us
    gather x1, local copies, waits for them, and re-layouts, shards(): up_pairs = jnp.take(up_all, up_table, axis=0)  7.67 us
    another operation x3, other arithmetic, orthonormal(): factor_low = jnp.linalg.cholesky(gram_mat)  6.52 us
  transfers between devices with their start and end apart: 2, of which 2 were waited for; matrix products, arithmetic and copies ran while one was open for 9% of the time, Pallas kernels for 0%

commit v1 on v0

--- a/solution.py
+++ b/solution.py
@@ -49,7 +49,9 @@
     up_local = up_store[0, 0]
     left_table = left_home[0, 0]
     up_table = up_home[0, 0]
-    left_all = lax.all_gather(left_local, "col", axis=0, tiled=True)
+    left_all = jnp.concatenate(
+        lax.all_to_all(jnp.stack([left_local] * lax.axis_size("col")), "col", 0, 0), axis=0
+    )
     up_all = lax.all_gather(up_local, "row", axis=0, tiled=True)
     left_pairs = jnp.take(left_all, left_table, axis=0)
     up_pairs = jnp.take(up_all, up_table, axis=0)

time: 274 us -> 456 us (1.66)
  waiting for transfers between devices: 175 us -> 340 us
  starting transfers between devices: 0.08 us -> 16 us
  local copies, waits for them, and re-layouts: 26.7 us -> 31.7 us
    all_to_all x0 -> x1, waiting for transfers between devices: none -> 249 us  [shards(): lax.all_to_all(jnp.stack([left_local] * lax.axis_size('col')), 'col', 0, 0)]
    all_gather x1 -> x0, waiting for transfers between devices: 109 us -> none  [shards(): left_all = lax.all_gather(left_local, 'col', axis=0, tiled=True)]
    all_gather x1, waiting for transfers between devices: 65 us -> 90.5 us  [shards(): up_all = lax.all_gather(up_local, 'row', axis=0, tiled=True)]
    all_to_all x0 -> x1, starting transfers between devices: none -> 15.9 us  [shards(): lax.all_to_all(jnp.stack([left_local] * lax.axis_size('col')), 'col', 0, 0)]
    another operation x0 -> x1, local copies, waits for them, and re-layouts: none -> 5.38 us  [shards(): jnp.stack([left_local] * lax.axis_size('col'))]
  transfers between devices with their start and end apart: 2 -> 2, of which waited for: 2 -> 2; matrix products, arithmetic and copies ran while one was open for 9% -> 5% of each run, Pallas kernels for 0% -> 0%
where the time goes in v1:
time: 456 us
  waiting for transfers between devices  340 us (75%)
  other arithmetic  33.6 us (7%)
  local copies, waits for them, and re-layouts  31.7 us (7%)
  starting transfers between devices  16 us (4%)
  between operations  14.3 us (3%)
  blocking collectives  13.5 us (3%)
  matrix products  7.07 us (2%)
    all_to_all x1, waiting for transfers between devices, shards(): lax.all_to_all(jnp.stack([left_local] * lax.axis_size('col')), 'col', 0, 0)  249 us
    all_gather x1, waiting for transfers between devices, shards(): up_all = lax.all_gather(up_local, 'row', axis=0, tiled=True)  90.5 us
    all_to_all x1, starting transfers between devices, shards(): lax.all_to_all(jnp.stack([left_local] * lax.axis_size('col')), 'col', 0, 0)  15.9 us
    all_to_all x2, blocking collectives, sent_and_summed(): lax.all_to_all(split_up(shard, dim, devices), axis, 0, 0, tiled=True)  9.33 us
  transfers between devices with their start and end apart: 2, of which 2 were waited for; matrix products, arithmetic and copies ran while one was open for 5% of the time, Pallas kernels for 0%

profile of v1, /device:TPU:1, one launch (start us, length us, event | category | flops | bytes accessed | tf_op | source)
XLA Modules:
  0.0 455.8 jit_solution(13733772855081996594)
XLA Ops:
  7.2 0.0 copy-start
  7.2 5.4 %stack.3 = f32[16,1,2,64,1024]{4,3,2,1,0:T(8,128)} broadcast(f32[2,64,1024]{2,1,0:T(8,128)} %bitcast.98), dimensions={2,3,4} | broadcast | bytes 8912896 | tf_op jit(solution)/shard_map/stack | solution.py:53
  12.6 0.0 copy-start.4
  12.6 0.0 copy-start.3
  12.6 0.0 copy-start.5
  12.6 15.9 %all-to-all-start = ((f32[16,1,2,64,1024]{4,3,2,1,0:T(8,128)}), f32[16,1,2,64,1024]{4,3,2,1,0:T(8,128)}, u32[]{:S(2)}, u32[]{:S(2)}) async-start(f32[16,1,2,64,1024]{4,3,2,1,0:T(8,128)} %stack.3), calls=%async_computation | async-start | bytes 16777216 | tf_op jit(solution)/shard_map/all_to_all | solution.py:53
  28.5 0.0 all-gather.3.cloned.1.call-start
  28.5 0.7 all-gather.3.cloned.1.call-update
  29.2 0.0 copy-done.4
  29.3 0.0 copy-done.3
  29.3 0.0 copy-done.5
  29.4 90.5 %all-gather.3.cloned.1.call-done = f32[16,1,1,2,64,1024]{5,4,3,2,1,0:T(8,128)} async-done(((f32[1,1,1,2,64,1024]{5,4,3,2,1,0:T(8,128)}), f32[16,1,1,2,64,1024]{5,4,3,2,1,0:T(8,128)}) %all-gather.3.cloned.1.call-update) | async-done | bytes 8388624 | tf_op jit(solution)/shard_map/all_gather | solution.py:55
  119.9 7.7 %gather_fusion = f32[16,2,64,1024]{3,2,1,0:T(8,128)} fusion(f32[16,2,64,1024]{3,2,1,0:T(8,128)} %bitcast.97, s32[1024]{0:T(1024)S(1)} %pad_clamp_fusion.3), kind=kCustom, calls=%fused_computation.clone | custom fusion | bytes 16777280 | tf_op jit(solution)/shard_map/jit(_take)/gather | solution.py:57
  127.5 8.6 %broadcast_select_fusion.1 = f32[16,2,64,1024]{3,2,1,0:T(8,128)} fusion(f32[16,2,64,1024]{3,2,1,0:T(8,128)} %gather_fusion, pred[16]{0:T(512)(128)(4,1)S(1)} %compare_and_fusion.3), kind=kLoop, calls=%fused_computation.5 | loop fusion | flops 2097152 | bytes 16777232 | tf_op jit(solution)/shard_map/jit(_take)/select_n | solution.py:57
  136.1 5.4 %gather_fusion.1 = f32[2,2,2,64,1024]{4,3,2,1,0:T(8,128)} fusion(f32[8,2,2,64,1024]{4,3,2,1,0:T(8,128)} %bitcast.95, s32[1024]{0:T(1024)S(1)} %pad_clamp_fusion.2), kind=kCustom, calls=%fused_computation.1.clone | custom fusion | bytes 4194312 | tf_op jit(solution)/shard_map/jit(_take)/gather | solution.py:62
  141.5 248.6 %all-to-all-done = f32[16,1,2,64,1024]{4,3,2,1,0:T(8,128)} async-done(((f32[16,1,2,64,1024]{4,3,2,1,0:T(8,128)}), f32[16,1,2,64,1024]{4,3,2,1,0:T(8,128)}, u32[]{:S(2)}, u32[]{:S(2)}) %all-to-all-start) | async-done | bytes 8388640 | tf_op jit(solution)/shard_map/all_to_all | solution.py:53
  390.1 7.7 %gather_fusion.2 = f32[16,2,64,1024]{3,2,1,0:T(8,128)} fusion(f32[16,2,64,1024]{3,2,1,0:T(8,128)} %bitcast.10, s32[1024]{0:T(1024)S(1)} %pad_clamp_fusion.1), kind=kCustom, calls=%fused_computation.2.clone | custom fusion | bytes 16777280 | tf_op jit(solution)/shard_map/jit(_take)/gather | solution.py:56
  397.8 8.6 %broadcast_select_fusion = f32[16,2,64,1024]{3,2,1,0:T(8,128)} fusion(f32[16,2,64,1024]{3,2,1,0:T(8,128)} %gather_fusion.2, pred[16]{0:T(512)(128)(4,1)S(1)} %compare_and_fusion.1), kind=kLoop, calls=%fused_computation.4 | loop fusion | flops 2097152 | bytes 16777232 | tf_op jit(solution)/shard_map/jit(_take)/select_n | solution.py:56
  406.4 5.4 %gather_fusion.3 = f32[2,2,2,64,1024]{4,3,2,1,0:T(8,128)} fusion(f32[8,2,2,64,1024]{4,3,2,1,0:T(8,128)} %bitcast.96, s32[1024]{0:T(1024)S(1)} %pad_clamp_fusion), kind=kCustom, calls=%fused_computation.3.clone | custom fusion | bytes 4194312 | tf_op jit(solution)/shard_map/jit(_take)/gather | solution.py:61
  411.8 2.8 copy_select_fusion
  414.6 0.0 copy-start.1
  414.6 0.0 copy-done
  414.6 1.6 fusion.1
  416.2 1.1 fusion
  417.3 0.3 fusion.9
  417.6 0.0 copy-done.1
  417.7 0.7 convolution_bitcast_fusion.1
  418.3 5.2 %all_to_all.20 = f32[2,1,64,1024]{3,2,1,0:T(8,128)S(1)} all-to-all(f32[2,1,64,1024]{3,2,1,0:T(8,128)S(1)} %convolution_bitcast_fusion.1), channel_id=1, replica_groups=mesh['row'=16,'col'=16,'depth'=2] {'depth'}, dimensions={0} | all-to-all | bytes 1048576 | tf_op jit(solution)/shard_map/all_to_all | solution.py:19
  423.6 0.4 fusion.10
  423.9 0.1 copy.27
  424.0 5.8 %custom-call.7 = f32[1,64,64]{2,1,0:T(8,128)S(1)} custom-call(f32[1,64,64]{2,1,0:T(8,128)S(1)} %fusion.6), custom_call_target="Cholesky" | custom-call | tf_op jit(solution)/shard_map/jit(cholesky)/cholesky | solution.py:42
  429.9 0.6 compare_reduce_fusion
  430.5 0.7 fusion.5
  431.2 4.9 %custom-call.8 = f32[1,1,64,64]{2,3,1,0:T(8,128)S(1)} custom-call(f32[1,1,64,64]{3,2,1,0:T(8,128)S(1)} %fusion.5), custom_call_target="InvertDiagBlocksLowerTriangular" | custom-call | tf_op jit(solution)/shard_map/triangular_solve | solution.py:43
  436.1 0.0 copy-start.2
  436.1 0.4 fusion.7
  436.5 0.7 multiply_bitcast_fusion.1
  437.3 4.2 all_to_all.21
  441.5 0.0 copy-done.2
  441.5 1.6 fusion.2
  443.1 0.3 fusion.11
  443.4 0.7 convolution_bitcast_fusion
  444.1 4.2 all_to_all.22
  448.2 0.7 multiply_bitcast_fusion
  (14 shorter events, 0.2 us)
Async XLA Ops:
  7.2 407.4 %copy-start = (f32[1,1,2,64,1024]{4,3,2,1,0:T(8,128)S(1)}, f32[1,1,2,64,1024]{4,3,2,1,0:T(8,128)}, u32[]{:S(2)}) copy-start(f32[1,1,2,64,1024]{4,3,2,1,0:T(8,128)} %param.15) | copy-start | bytes 1572868
  12.6 16.7 %copy-start.4 = (s32[1,1,16]{2,1,0:T(1,128)S(1)}, s32[1,1,16]{2,1,0:T(1,128)}, u32[]{:S(2)}) copy-start(s32[1,1,16]{2,1,0:T(1,128)} %param.11) | copy-start | bytes 196
  12.6 16.7 %copy-start.3 = (s32[1,1,2]{2,1,0:T(1,128)S(1)}, s32[1,1,2]{2,1,0:T(1,128)}, u32[]{:S(2)}) copy-start(s32[1,1,2]{2,1,0:T(1,128)} %param.14) | copy-start | bytes 28
  12.6 16.7 %copy-start.5 = (s32[1,1,16]{2,1,0:T(1,128)S(1)}, s32[1,1,16]{2,1,0:T(1,128)}, u32[]{:S(2)}) copy-start(s32[1,1,16]{2,1,0:T(1,128)} %param.13) | copy-start | bytes 196
  12.6 377.5 %all-to-all-start = ((f32[16,1,2,64,1024]{4,3,2,1,0:T(8,128)}), f32[16,1,2,64,1024]{4,3,2,1,0:T(8,128)}, u32[]{:S(2)}, u32[]{:S(2)}) async-start(f32[16,1,2,64,1024]{4,3,2,1,0:T(8,128)} %stack.3), calls=%async_computation | async-start | bytes 16777216 | tf_op jit(solution)/shard_map/all_to_all | solution.py:53
  28.5 91.4 %all-gather.3.cloned.1.call-start = ((), (), s32[]{:S(2)}) async-start(), calls=%async_computation.4 | async-start | bytes 8912896 | tf_op jit(solution)/shard_map/all_gather | solution.py:55
  414.6 3.1 copy-start.1
  436.1 5.4 %copy-start.2 = (f32[2,2,2,64,1024]{4,3,1,0,2:T(8,128)S(1)}, f32[2,2,2,64,1024]{4,3,1,0,2:T(8,128)}, u32[]{:S(2)}) copy-start(f32[2,2,2,64,1024]{4,3,1,0,2:T(8,128)} %copy-done.1) | copy-start | bytes 6291460
Sparse Core Ops, SparseCore 0:
  32.3 87.5 all-gather.2
